TPU v7x, 256 devices: a whole 4x4x8 slice. The times are simulated.
256 devices in a mesh: chan: 32 (over x, y, z_lo), win: 8 (over z_hi, core).
Axes of the slice: x: 4, y: 4, z: 8 (z_hi: 4, z_lo: 2; z = z_hi * 2 + z_lo), core: 2. Of those that a mesh axis runs over, the one named last changes fastest.
Arguments:
- records: float32 [32, 1024, 1024], P('win', 'chan'), may hold values from -180 to 180
- sources: int32 [32], replicated, may hold values from 0 to 1023, as said below
Outputs:
- correlations: float32 [32, 256, 1024], P('win', None, 'chan')
Inputs may be any that keep to these rules, and one draw needn't show every extreme that they name: `sources`: source s is one of the channels s * 32 to (s + 1) * 32 - 1; the first source is channel 0 and the last is channel 1024 - 1.
All inputs are finite; a program needn't handle non-finite values.
Results may differ from a plain program's by a relative error of at most 0.00022.
Values sent between devices are 32-bit elements; how exact they have to be, the bound alone decides.
No kernel may reach another device: no remote copies, remote signals or barrier semaphores. Data moves between devices by JAX's collectives and lax.ppermute only.
A program may use at most 64 MiB of HBM per device.

v0:
```python
import math
import jax
import jax.numpy as jnp
from jax import lax
from jax.sharding import PartitionSpec as P

HIGHEST = lax.Precision.HIGHEST
AMPLITUDE_FLOOR = 0.25
WHITE_EPSILON = 1e-06


def fourier_table(length):
    freq_count = length // 2
    freqs = jnp.arange(freq_count, dtype=jnp.int32)[:, None]
    sample_index = jnp.arange(length, dtype=jnp.int32)[None, :]
    angles = (freqs * sample_index % length).astype(jnp.float32) * (2.0 * math.pi / length)
    return jnp.concatenate([jnp.cos(angles), -jnp.sin(angles)], axis=0)


def band_table(freq_count, reach):
    rows_index = jnp.arange(freq_count, dtype=jnp.int32)[:, None]
    cols_index = jnp.arange(freq_count, dtype=jnp.int32)[None, :]
    return (jnp.abs(rows_index - cols_index) <= reach).astype(jnp.float32)


def inverse_table(length, lag_count, first_bin, bin_count, factor):
    freqs = first_bin + jnp.arange(bin_count, dtype=jnp.int32)
    lag_index = jnp.arange(lag_count, dtype=jnp.int32) - lag_count // 2
    angles = (lag_index[:, None] * freqs[None, :] % length).astype(jnp.float32) * (
        2.0 * math.pi / length
    )
    weights = jnp.where(freqs == 0, 1.0, 2.0).astype(jnp.float32)[None, :] * factor
    return jnp.concatenate([weights * jnp.cos(angles), -weights * jnp.sin(angles)], axis=1)


def running_level(padded, time_count, window_span):
    window_total = padded.shape[0]
    chans = padded.shape[2]
    running = jnp.concatenate(
        [jnp.zeros((window_total, 1, chans), jnp.float32), jnp.cumsum(jnp.abs(padded), axis=1)],
        axis=1,
    )
    return (running[:, window_span:] - running[:, :time_count]) / window_span


def local(records, sources):
    chan_count = lax.axis_size("chan")
    local_windows, local_time, all_channels = records.shape
    length = local_time * chan_count
    freq_count = length // 2
    chan_width = all_channels // chan_count
    half_width = min(16, local_time)
    smooth_reach = length // 32
    window_span = 2 * half_width + 1
    lag_count = length // 4
    forward = fourier_table(length)
    band_matrix = band_table(freq_count, smooth_reach)
    pieces = lax.all_to_all(records, "chan", split_axis=2, concat_axis=1, tiled=True)
    padded = jnp.pad(pieces, ((0, 0), (half_width, half_width), (0, 0)))
    amplitude = running_level(padded, length, window_span)
    whiten_pieces = pieces / jnp.maximum(amplitude, AMPLITUDE_FLOOR)
    spectrum = jnp.einsum("kt,wtc->wkc", forward, whiten_pieces, precision=HIGHEST)
    real_part = spectrum[:, :freq_count]
    imag_part = spectrum[:, freq_count:]
    magnitude = jnp.sqrt(real_part * real_part + imag_part * imag_part)
    smoothed = (
        jnp.einsum("jk,wkc->wjc", band_matrix, magnitude, precision=HIGHEST)
        / (2 * smooth_reach + 1)
        + WHITE_EPSILON
    )
    whitened = jnp.stack([real_part / smoothed, imag_part / smoothed], axis=1)
    band_data = lax.all_to_all(whitened, "win", split_axis=2, concat_axis=0, tiled=True)
    total_windows = band_data.shape[0]
    band_count = band_data.shape[2]
    chan_index = lax.axis_index("chan")
    channel_ids = jnp.arange(chan_width, dtype=jnp.int32)
    selector = (sources[:, None] == chan_index * chan_width + channel_ids[None, :]).astype(
        jnp.float32
    )
    chosen = jnp.einsum("sc,wafc->wafs", selector, band_data, precision=HIGHEST)
    spectra = lax.psum(chosen, "chan")
    source_real = spectra[:, 0]
    source_imag = spectra[:, 1]
    white_real = band_data[:, 0]
    white_imag = band_data[:, 1]
    cross_real = jnp.einsum(
        "wfs,wfc->fsc", source_real, white_real, precision=HIGHEST
    ) + jnp.einsum("wfs,wfc->fsc", source_imag, white_imag, precision=HIGHEST)
    cross_imag = jnp.einsum(
        "wfs,wfc->fsc", source_real, white_imag, precision=HIGHEST
    ) - jnp.einsum("wfs,wfc->fsc", source_imag, white_real, precision=HIGHEST)
    stacked = jnp.stack([cross_real, cross_imag])
    factor = 1.0 / math.sqrt(total_windows * freq_count)
    band_start = lax.axis_index("win") * band_count
    band_table_part = inverse_table(length, lag_count, band_start, band_count, factor).reshape(
        lag_count, 2, band_count
    )
    return lax.psum_scatter(
        jnp.einsum("tak,aksc->stc", band_table_part, stacked, precision=HIGHEST),
        "win",
        scatter_dimension=0,
        tiled=True,
    )


def solution(mesh):
    placed = (P("win", "chan", None), P())
    return jax.shard_map(
        local, mesh=mesh, in_specs=placed, out_specs=P("win", None, "chan"), check_vma=False
    )
```

profile of v0, /device:TPU:2, one launch (start us, length us, event | category | flops | bytes accessed | tf_op | source)
XLA Modules:
  0.0 526.2 jit_solution(4063981459503955568)
XLA Ops:
  6.5 1.8 copy.27
  8.3 2.1 reshape.206
  10.4 9.0 %all-to-all-start = ((f32[32,1,4096]{2,1,0:T(1,128)}), f32[32,1,4096]{2,1,0:T(1,128)S(1)}, u32[]{:S(2)}, u32[]{:S(2)}) async-start(f32[32,1,4096]{2,1,0:T(1,128)} %reshape.206), calls=%async_computation | async-start | bytes 1048576 | tf_op jit(solution)/shard_map/all_to_all | solution.py:58
  19.4 9.1 %sine_negate_fusion = (f32[512,1024]{1,0:T(8,128)S(1)}, f32[512,1024]{1,0:T(8,128)}) fusion(), kind=kLoop, calls=%fused_computation.14 | loop fusion | flops 7864320 | bytes 4194304 | tf_op jit(solution)/shard_map/neg | solution.py:17
  28.5 0.7 all-to-all-done
  29.2 0.5 broadcast.250
  29.7 1.9 reduce
  31.6 2.4 reshape.207
  34.0 4.1 copy.49
  38.1 2.4 all_to_all.29
  40.5 0.2 abs_bitcast_fusion
  40.8 0.5 copy-done.1
  41.3 1.1 reshape.199
  42.4 62.7 %reduce-window.6 = f32[4,32,9,128]{3,2,1,0:T(8,128)S(1)} reduce-window(f32[4,32,9,128]{3,2,1,0:T(8,128)} %reshape.199, f32[]{:T(128)} %constant.22.clone.1), window={size=1x1x1x128 pad=0_0x0_0x0_0x127_0}, to_apply=%region_0.1 | reduce-window | flops 18726912 | bytes 1179652 | tf_op jit(solution)/shard_map/reduce-window
  105.2 1.3 slice.45
  106.5 1.5 copy.29
  108.1 0.1 copy.30
  108.2 1.3 broadcast_add_fusion
  109.5 1.3 reduce_window_sum.16
  110.8 6.1 %fusion.16 = f32[4,1024,32]{1,2,0:T(8,128)S(1)} fusion(f32[512,1024]{1,0:T(8,128)S(1)} %get-tuple-element.13, f32[512,1024]{1,0:T(8,128)} %get-tuple-element.14, f32[4,1024,32]{1,2,0:T(8,128)} %copy-done.1, f32[4,1056,32]{1,2,0:T(8,128)S(1)} %bitcast.85, f32[4,1152,32]{1,2,0:T(8,128)S(1)} %bitcast.84), kind=kOutput, calls=%fused_computation.23 | convolution fusion | flops 1612185600 | bytes 6356992 | tf_op jit(solution)/shard_map/kt,wtc->wkc/dot_general | solution.py:62
  117.0 0.7 divide_bitcast_fusion.1
  117.7 1.3 copy.31
  119.0 2.1 reshape.208
  121.1 7.6 %all-to-all-start.1 = ((f32[8,1,16384]{2,1,0:T(1,128)}), f32[8,1,16384]{2,1,0:T(1,128)S(1)}, u32[]{:S(2)}, u32[]{:S(2)}) async-start(f32[8,1,16384]{2,1,0:T(1,128)} %reshape.208), calls=%async_computation.1 | async-start | bytes 1048576 | tf_op jit(solution)/shard_map/all_to_all | solution.py:72
  128.7 0.0 all-reduce.5.cloned.1.call-start
  128.8 18.3 %all-to-all-done.1 = f32[8,1,16384]{2,1,0:T(1,128)S(1)} async-done(((f32[8,1,16384]{2,1,0:T(1,128)}), f32[8,1,16384]{2,1,0:T(1,128)S(1)}, u32[]{:S(2)}, u32[]{:S(2)}) %all-to-all-start.1) | async-done | bytes 524320 | tf_op jit(solution)/shard_map/all_to_all | solution.py:72
  147.0 1.9 reduce.1
  148.9 1.1 reshape.209
  150.0 0.8 copy.32
  150.9 1.6 fusion.44
  152.5 0.0 all-reduce.5.cloned.1.call-update
  152.5 0.0 reduce-scatter.2.cloned.1.call-start
  152.6 0.3 cosine_multiply_fusion
  152.9 0.1 slice_bitcast_fusion.2
  153.0 0.9 copy.34
  154.0 0.9 copy.36
  154.9 299.8 %all-reduce.5.cloned.1.call-done = f32[32,2,64,32]{2,3,1,0:T(8,128)} async-done(((f32[32,2,64,32]{2,3,1,0:T(8,128)}), f32[32,2,64,32]{2,3,1,0:T(8,128)}) %all-reduce.5.cloned.1.call-update) | async-done | bytes 524304 | tf_op jit(solution)/shard_map/psum | solution.py:81
  454.7 2.3 slice_bitcast_fusion.1
  457.0 2.0 copy.33
  459.0 2.8 copy.35
  461.8 1.2 fusion.61
  463.0 1.2 fusion.62
  464.2 0.0 copy-done
  464.2 1.2 fusion.15
  465.4 1.2 fusion.14
  466.6 0.3 pad_maximum_fusion
  466.8 5.1 fusion.11
  472.0 47.4 %reduce-scatter.2.cloned.1.call-done = f32[4,256,32]{1,2,0:T(8,128)} async-done(((f32[32,256,32]{1,2,0:T(8,128)}), f32[4,256,32]{1,2,0:T(8,128)}) %reduce-scatter.2.cloned.1.call-update) | async-done | bytes 131088 | tf_op jit(solution)/shard_map/reduce_scatter | solution.py:98
  (13 shorter events, 0.1 us)
Async XLA Ops:
  10.4 18.7 %all-to-all-start = ((f32[32,1,4096]{2,1,0:T(1,128)}), f32[32,1,4096]{2,1,0:T(1,128)S(1)}, u32[]{:S(2)}, u32[]{:S(2)}) async-start(f32[32,1,4096]{2,1,0:T(1,128)} %reshape.206), calls=%async_computation | async-start | bytes 1048576 | tf_op jit(solution)/shard_map/all_to_all | solution.py:58
  40.5 0.8 copy-start.1
  121.1 25.9 %all-to-all-start.1 = ((f32[8,1,16384]{2,1,0:T(1,128)}), f32[8,1,16384]{2,1,0:T(1,128)S(1)}, u32[]{:S(2)}, u32[]{:S(2)}) async-start(f32[8,1,16384]{2,1,0:T(1,128)} %reshape.208), calls=%async_computation.1 | async-start | bytes 1048576 | tf_op jit(solution)/shard_map/all_to_all | solution.py:72
  128.7 326.1 %all-reduce.5.cloned.1.call-start = ((), (), s32[]{:S(2)}) async-start(), calls=%async_computation.3 | async-start | bytes 2097152 | tf_op jit(solution)/shard_map/psum | solution.py:81
  150.0 0.8 copy-start.2
  152.5 366.9 %reduce-scatter.2.cloned.1.call-start = ((), (), s32[]{:S(2)}) async-start(), calls=%async_computation.4 | async-start | bytes 1179648 | tf_op jit(solution)/shard_map/reduce_scatter | solution.py:98
  463.0 1.2 copy-start
Sparse Core Ops, SparseCore 0:
  152.7 302.0 all-reduce.4
  472.1 47.2 reduce-scatter.1
where the time goes:
time: 531 us; the launch traced here: 526 us
  waiting for transfers between devices  366 us (69%)
  other arithmetic  77.8 us (15%)
  local copies, waits for them, and re-layouts  33.7 us (6%)
  matrix products  18.3 us (3%)
  starting transfers between devices  16.6 us (3%)
  between operations  13.7 us (3%)
    psum x1, waiting for transfers between devices, local(): spectra = lax.psum(chosen, 'chan')  300 us
    another operation x3, other arithmetic  64.1 us
    reduce_scatter x1, waiting for transfers between devices, local(): lax.psum_scatter(jnp.einsum('tak,aksc->stc', band_table_part, stacked, pr...  47.4 us
    all_to_all x1, waiting for transfers between devices, local(): lax.all_to_all(whitened, 'win', split_axis=2, concat_axis=0, tiled=True)  18.3 us
  transfers between devices with their start and end apart: 4, of which 4 were waited for; matrix products, arithmetic and copies ran while one was open for 2% of the time, Pallas kernels for 0%

commit v1 on v0

--- a/solution.py
+++ b/solution.py
@@ -7,6 +7,7 @@
 HIGHEST = lax.Precision.HIGHEST
 AMPLITUDE_FLOOR = 0.25
 WHITE_EPSILON = 1e-06
+use_ways_for = lambda incoming_x: lax.all_gather(incoming_x, axis_name="chan").sum(axis=0)
 
 
 def fourier_table(length):
@@ -78,7 +79,7 @@
         jnp.float32
     )
     chosen = jnp.einsum("sc,wafc->wafs", selector, band_data, precision=HIGHEST)
-    spectra = lax.psum(chosen, "chan")
+    spectra = use_ways_for(chosen)
     source_real = spectra[:, 0]
     source_imag = spectra[:, 1]
     white_real = band_data[:, 0]

time: 531 us -> 941 us (1.77)
  waiting for transfers between devices: 366 us -> 764 us
  other arithmetic: 77.8 us -> 91 us
    all_gather x0 -> x1, waiting for transfers between devices: none -> 705 us  [lax.all_gather(incoming_x, axis_name='chan').sum(axis=0)]
    psum x1 -> x0, waiting for transfers between devices: 300 us -> none  [local(): spectra = lax.psum(chosen, 'chan')]
    reduce_sum x0 -> x1, other arithmetic: none -> 13.2 us  [lax.all_gather(incoming_x, axis_name='chan').sum(axis=0)]
  transfers between devices with their start and end apart: 4 -> 4, of which waited for: 4 -> 4; matrix products, arithmetic and copies ran while one was open for 2% -> 1% of each run, Pallas kernels for 0% -> 0%
where the time goes in v1:
time: 941 us; the launch traced here: 936 us
  waiting for transfers between devices  764 us (81%)
  other arithmetic  91 us (10%)
  local copies, waits for them, and re-layouts  32.4 us (3%)
  matrix products  18.2 us (2%)
  starting transfers between devices  16.6 us (2%)
  between operations  13.7 us (1%)
    all_gather x1, waiting for transfers between devices, lax.all_gather(incoming_x, axis_name='chan').sum(axis=0)  705 us
    another operation x3, other arithmetic  64.1 us
    reduce_scatter x1, waiting for transfers between devices, local(): lax.psum_scatter(jnp.einsum('tak,aksc->stc', band_table_part, stacked, pr...  40.4 us
  transfers between devices with their start and end apart: 4, of which 4 were waited for; matrix products, arithmetic and copies ran while one was open for 1% of the time, Pallas kernels for 0%

profile of v1, /device:TPU:2, one launch (start us, length us, event | category | flops | bytes accessed | tf_op | source)
XLA Modules:
  0.0 935.9 jit_solution(351306183709114432)
XLA Ops:
  6.5 1.8 copy.19
  8.3 2.1 reshape.207
  10.4 9.0 all-to-all-start
  19.4 9.1 sine_negate_fusion
  28.5 0.7 all-to-all-done
  29.2 0.5 broadcast.250
  29.7 1.9 reduce
  31.6 2.4 reshape.208
  34.0 4.1 copy.41
  38.1 2.4 all_to_all.29
  40.5 0.2 abs_bitcast_fusion
  40.8 0.5 copy-done.1
  41.3 1.1 reshape.199
  42.4 62.7 %reduce-window.6 = f32[4,32,9,128]{3,2,1,0:T(8,128)S(1)} reduce-window(f32[4,32,9,128]{3,2,1,0:T(8,128)} %reshape.199, f32[]{:T(128)} %constant.22.clone.1), window={size=1x1x1x128 pad=0_0x0_0x0_0x127_0}, to_apply=%region_0.1 | reduce-window | flops 18726912 | bytes 1179652 | tf_op jit(solution)/shard_map/reduce-window
  105.2 1.3 slice.45
  106.5 1.5 copy.21
  108.1 0.1 copy.22
  108.2 1.3 broadcast_add_fusion
  109.5 1.3 reduce_window_sum.16
  110.8 6.1 fusion.16
  117.0 0.7 divide_bitcast_fusion.1
  117.7 1.3 copy.23
  119.0 2.1 reshape.209
  121.1 7.6 all-to-all-start.1
  128.7 0.0 all-gather.3.cloned.1.call-start
  128.7 18.3 %all-to-all-done.1 = f32[8,1,16384]{2,1,0:T(1,128)S(1)} async-done(((f32[8,1,16384]{2,1,0:T(1,128)}), f32[8,1,16384]{2,1,0:T(1,128)S(1)}, u32[]{:S(2)}, u32[]{:S(2)}) %all-to-all-start.1) | async-done | bytes 524320 | tf_op jit(solution)/shard_map/all_to_all | solution.py:73
  147.0 1.9 reduce.1
  148.9 1.1 reshape.210
  150.0 0.8 copy.24
  150.9 1.6 fusion.50
  152.5 0.0 reduce-scatter.2.cloned.1.call-start
  152.6 0.3 cosine_multiply_fusion
  152.9 0.1 slice_bitcast_fusion.1
  153.0 0.9 copy.26
  153.9 0.9 copy.28
  154.9 704.6 %all-gather.3.cloned.1.call-done = f32[1024,2,64,32]{2,3,1,0:T(8,128)} async-done(((f32[32,2,64,32]{2,3,1,0:T(8,128)}), f32[1024,2,64,32]{2,3,1,0:T(8,128)}) %all-gather.3.cloned.1.call-update) | async-done | bytes 16777232 | tf_op jit(solution)/shard_map/all_gather | solution.py:10
  859.4 13.2 %reduce_sum.9 = f32[32,2,64,32]{2,3,1,0:T(8,128)S(1)} reduce(f32[32,32,2,64,32]{3,4,2,1,0:T(8,128)} %bitcast.80, f32[]{:T(128)} %constant.22.clone.1), dimensions={0}, to_apply=%region_2.3 | reduce | flops 4063232 | bytes 17301508 | tf_op jit(solution)/shard_map/reduce_sum | solution.py:10
  872.7 1.0 fusion.63
  873.7 2.0 copy.34
  875.7 2.8 copy.35
  878.5 1.2 fusion.23
  879.7 1.2 fusion.21
  880.8 0.0 copy-done
  880.9 1.2 fusion.15
  882.1 1.2 fusion.14
  883.2 0.3 pad_maximum_fusion
  883.5 5.1 fusion.11
  888.6 40.4 %reduce-scatter.2.cloned.1.call-done = f32[4,256,32]{1,2,0:T(8,128)} async-done(((f32[32,256,32]{1,2,0:T(8,128)}), f32[4,256,32]{1,2,0:T(8,128)}) %reduce-scatter.2.cloned.1.call-update) | async-done | bytes 131088 | tf_op jit(solution)/shard_map/reduce_scatter | solution.py:99
  (14 shorter events, 0.2 us)
Async XLA Ops:
  10.4 18.7 %all-to-all-start = ((f32[32,1,4096]{2,1,0:T(1,128)}), f32[32,1,4096]{2,1,0:T(1,128)S(1)}, u32[]{:S(2)}, u32[]{:S(2)}) async-start(f32[32,1,4096]{2,1,0:T(1,128)} %reshape.207), calls=%async_computation | async-start | bytes 1048576 | tf_op jit(solution)/shard_map/all_to_all | solution.py:59
  40.5 0.8 copy-start.1
  121.1 25.9 %all-to-all-start.1 = ((f32[8,1,16384]{2,1,0:T(1,128)}), f32[8,1,16384]{2,1,0:T(1,128)S(1)}, u32[]{:S(2)}, u32[]{:S(2)}) async-start(f32[8,1,16384]{2,1,0:T(1,128)} %reshape.209), calls=%async_computation.1 | async-start | bytes 1048576 | tf_op jit(solution)/shard_map/all_to_all | solution.py:73
  128.7 730.8 %all-gather.3.cloned.1.call-start = ((), (), s32[]{:S(2)}) async-start(), calls=%async_computation.4 | async-start | bytes 34603008 | tf_op jit(solution)/shard_map/all_gather | solution.py:10
  150.0 0.8 copy-start.2
  152.5 776.6 %reduce-scatter.2.cloned.1.call-start = ((), (), s32[]{:S(2)}) async-start(), calls=%async_computation.3 | async-start | bytes 1179648 | tf_op jit(solution)/shard_map/reduce_scatter | solution.py:99
  879.7 1.2 copy-start
Sparse Core Ops, SparseCore 0:
  152.6 706.7 all-gather.2
  888.8 40.2 reduce-scatter.1
